TPU v7x, 32 devices: a whole 2x2x4 slice. The times are simulated.
32 devices in a mesh: grp: 2 (over x), row: 16 (over z, y, core).
Axes of the slice: x: 2, y: 2, z: 4, core: 2. Of those that a mesh axis runs over, the one named last changes fastest.
Arguments:
- coupling_features: bfloat16 [1024, 512, 128], P(('grp', 'row')), parts along dimension 0, may hold values from -6 to 6
- aligned_features: bfloat16 [256, 512, 256], P(('grp', 'row')), parts along dimension 0, may hold values from -6 to 6
- aligned_entry_flags: int32 [256, 512], P('grp'), parts along dimension 0, may hold values 0 or 1
- amino_real_flags: int32 [1024], P('grp'), parts along dimension 0, may hold values from 0 to 1, as said below
- coupling_offset_matrix: bfloat16 [128, 8], replicated, may hold values from -3.5 to 3.5
- lookup_matrices: bfloat16 [256, 1024], replicated, may hold values from -0.75 to 0.75
- aligned_final_matrix: bfloat16 [256, 256], replicated, may hold values from -0.375 to 0.375
- product_factor_matrices: bfloat16 [256, 64], replicated, may hold values from -0.375 to 0.375
- product_final_matrix: bfloat16 [1024, 128], replicated, may hold values from -1 to 1
- trio_factor_matrices: bfloat16 [128, 640], replicated, may hold values from -0.5 to 0.5
- trio_final_matrix: bfloat16 [128, 128], replicated, may hold values from -0.5 to 0.5
- feedforward_expand: bfloat16 [128, 512], replicated, may hold values from -0.5 to 0.5
- feedforward_shrink: bfloat16 [512, 128], replicated, may hold values from -0.25 to 0.25
Outputs:
- msa_out: bfloat16 [256, 512, 256], P(('grp', 'row')), parts along dimension 0
- coupling_refreshed: bfloat16 [1024, 512, 128], P(('grp', 'row')), parts along dimension 0
There are 2 independent parts, one for each index of `grp`. A program takes and returns all parts, laid end to end along the dimension named above; an argument that names none is the same for every part. Nothing has to cross between parts.
Inputs may be any that keep to these rules, and one draw needn't show every extreme that they name: `amino_real_flags`: 1 on a prefix of at least 256 residues and 0 on the rest, which is never empty.
All inputs are finite; a program needn't handle non-finite values.
Results may differ from a plain program's by a relative error of at most 0.008.
The roundings to bfloat16 on the way count: a program that leaves them out, or rounds other values in their place, can miss the bound.
Values may be sent and summed in bfloat16 or wider, within the bound.
No kernel may reach another device: no remote copies, remote signals or barrier semaphores. Data moves between devices by JAX's collectives and lax.ppermute only.
A program may use at most 192 MiB of HBM per device.

v0:
```python
import jax
import jax.numpy as jnp
from jax import lax
from jax.sharding import PartitionSpec as P

EPSILON = 1e-05


def standardize_features(values, dimension=-1):
    values = values.astype(jnp.float32)
    centered = values - jnp.mean(values, axis=dimension, keepdims=True)
    variance = jnp.mean(centered * centered, axis=dimension, keepdims=True)
    return centered * lax.rsqrt(variance + EPSILON)


def apply_matrix_map(values, weight):
    return jnp.einsum("...c,cd->...d", values, weight, preferred_element_type=jnp.float32)


def project_outer(raw_outer, product_final_matrix):
    row_total, col_total, left_width, right_width = raw_outer.shape
    flat = raw_outer.astype(jnp.bfloat16).reshape(row_total, col_total, left_width * right_width)
    return apply_matrix_map(flat, product_final_matrix)


def body(
    coupling_features,
    aligned_features,
    aligned_entry_flags,
    amino_real_flags,
    coupling_offset_matrix,
    lookup_matrices,
    aligned_final_matrix,
    product_factor_matrices,
    product_final_matrix,
    trio_factor_matrices,
    trio_final_matrix,
    feedforward_expand,
    feedforward_shrink,
):
    owned_aligned_lines = coupling_features.shape[0]
    residues = coupling_features.shape[1]
    pair_width = coupling_features.shape[2]
    owned_aligned_seqs = aligned_features.shape[0]
    aligned_feature_dim = aligned_features.shape[2]
    subspace_tally = coupling_offset_matrix.shape[1]
    subspace_dimension = aligned_feature_dim // subspace_tally
    outer_width = product_factor_matrices.shape[1] // 2
    placement_index = lax.axis_index("row")
    amino_real_valid = amino_real_flags.astype(jnp.float32)
    aligned_entry_valid = aligned_entry_flags.astype(jnp.float32) * amino_real_valid[None, :]
    my_residues = lax.dynamic_slice_in_dim(
        amino_real_valid, placement_index * owned_aligned_lines, owned_aligned_lines, 0
    )
    pair_valid = my_residues[:, None] * amino_real_valid[None, :]
    owned_aligned_flags = lax.dynamic_slice_in_dim(
        aligned_entry_valid, placement_index * owned_aligned_seqs, owned_aligned_seqs, 0
    )
    pair_normed = standardize_features(coupling_features).astype(jnp.bfloat16)
    bias_local = jnp.einsum(
        "ijc,ch->hij", pair_normed, coupling_offset_matrix, preferred_element_type=jnp.float32
    ).astype(jnp.bfloat16)
    tri_gates = jnp.einsum(
        "ijc,cd->dij",
        pair_normed,
        trio_factor_matrices[:, 0 : 4 * pair_width],
        preferred_element_type=jnp.float32,
    )
    left_tri = (
        jax.nn.sigmoid(tri_gates[0:pair_width])
        * tri_gates[pair_width : 2 * pair_width]
        * pair_valid[None]
    ).astype(jnp.bfloat16)
    right_tri = (
        jax.nn.sigmoid(tri_gates[2 * pair_width : 3 * pair_width])
        * tri_gates[3 * pair_width : 4 * pair_width]
        * pair_valid[None]
    ).astype(jnp.bfloat16)
    out_gate = jax.nn.sigmoid(
        apply_matrix_map(pair_normed, trio_factor_matrices[:, 4 * pair_width : 5 * pair_width])
    )
    left_full, right_full = (
        lax.all_to_all(left_tri, "row", split_axis=0, concat_axis=1, tiled=True),
        lax.all_to_all(right_tri, "row", split_axis=0, concat_axis=1, tiled=True),
    )
    tri_sum = jnp.einsum(
        "cik,cjk->cij", left_full, right_full, preferred_element_type=jnp.float32
    ).astype(jnp.bfloat16)
    tri_back = lax.all_to_all(tri_sum, "row", split_axis=1, concat_axis=0, tiled=True)
    tri_normed = standardize_features(tri_back, 0).astype(jnp.bfloat16)
    tri_update = out_gate * jnp.einsum(
        "cij,ce->ije", tri_normed, trio_final_matrix, preferred_element_type=jnp.float32
    )
    pair_one = coupling_features.astype(jnp.float32) + tri_update
    trans_hidden = jnp.maximum(
        apply_matrix_map(standardize_features(pair_one).astype(jnp.bfloat16), feedforward_expand),
        0.0,
    ).astype(jnp.bfloat16)
    pair_two = pair_one + apply_matrix_map(trans_hidden, feedforward_shrink)
    aligned_standardized = standardize_features(aligned_features).astype(jnp.bfloat16)
    lookup_factors_all = apply_matrix_map(aligned_standardized, lookup_matrices)
    asking_vectors = (
        (lookup_factors_all[..., 0:aligned_feature_dim] * subspace_dimension ** (-0.5))
        .astype(jnp.bfloat16)
        .reshape(owned_aligned_seqs, residues, subspace_tally, subspace_dimension)
    )
    lookup_subspaces = (
        lookup_factors_all[..., aligned_feature_dim : 2 * aligned_feature_dim]
        .astype(jnp.bfloat16)
        .reshape(owned_aligned_seqs, residues, subspace_tally, subspace_dimension)
    )
    content_subspaces = (
        lookup_factors_all[..., 2 * aligned_feature_dim : 3 * aligned_feature_dim]
        .astype(jnp.bfloat16)
        .reshape(owned_aligned_seqs, residues, subspace_tally, subspace_dimension)
    )
    aligned_sigmoid_factor = jax.nn.sigmoid(
        lookup_factors_all[..., 3 * aligned_feature_dim : 4 * aligned_feature_dim]
    )
    bias_piece = lax.all_gather(bias_local, "row", axis=1, tiled=True)
    asking_rows_sum = bias_piece.shape[1]
    affinity_matrix = jnp.einsum(
        "sihd,sjhd->shij", asking_vectors, lookup_subspaces, preferred_element_type=jnp.float32
    )
    affinity_matrix = affinity_matrix + bias_piece[None].astype(jnp.float32)
    affinity_matrix = jnp.where(
        owned_aligned_flags[:, None, None, :] > 0, affinity_matrix, -1000000000.0
    )
    attn_weights = jax.nn.softmax(affinity_matrix, axis=-1).astype(jnp.bfloat16)
    combined_features = jnp.einsum(
        "shij,sjhd->sihd", attn_weights, content_subspaces, preferred_element_type=jnp.float32
    )
    softmax_mixed_result = (
        combined_features.reshape(owned_aligned_seqs, asking_rows_sum, aligned_feature_dim)
        * aligned_sigmoid_factor
    ).astype(jnp.bfloat16)
    aligned_refreshed = aligned_features.astype(jnp.float32) + apply_matrix_map(
        softmax_mixed_result, aligned_final_matrix
    )
    product_standardized = standardize_features(aligned_refreshed).astype(jnp.bfloat16)
    product_factors = (
        jnp.einsum(
            "slm,mc->scl",
            product_standardized,
            product_factor_matrices,
            preferred_element_type=jnp.float32,
        )
        * owned_aligned_flags[:, None, :]
    )
    left_opm = product_factors[:, 0:outer_width].astype(jnp.bfloat16)
    right_opm = product_factors[:, outer_width : 2 * outer_width].astype(jnp.bfloat16)
    owned_crop_sites = lax.dynamic_slice_in_dim(
        aligned_entry_valid, placement_index * owned_aligned_lines, owned_aligned_lines, 1
    )
    coupling_tally = jnp.dot(
        owned_crop_sites.T, aligned_entry_valid, precision=lax.Precision.HIGHEST
    )
    left_res = lax.all_to_all(left_opm, "row", split_axis=2, concat_axis=0, tiled=True)
    right_all = lax.all_gather(right_opm, "row", axis=0, tiled=True)
    raw_total = jnp.einsum("sci,sdj->ijcd", left_res, right_all, preferred_element_type=jnp.float32)
    opm_sum = project_outer(raw_total, product_final_matrix)
    coupling_refreshed = (pair_two + opm_sum / jnp.maximum(coupling_tally, 1.0)[..., None]).astype(
        jnp.bfloat16
    )
    return (aligned_refreshed.astype(jnp.bfloat16), coupling_refreshed)


def solution(mesh):
    return jax.shard_map(
        body,
        mesh=mesh,
        in_specs=(
            P(("grp", "row"), None, None),
            P(("grp", "row"), None, None),
            P("grp", None),
            P("grp"),
            P(),
            P(),
            P(),
            P(),
            P(),
            P(),
            P(),
            P(),
            P(),
        ),
        out_specs=(P(("grp", "row"), None, None), P(("grp", "row"), None, None)),
        check_vma=False,
    )
```

profile of v0, /device:TPU:13, one launch (start us, length us, event | category | flops | bytes accessed | tf_op | source)
XLA Modules:
  0.0 526.1 jit_solution(14875835274564698252)
XLA Ops:
  7.2 6.5 %copy.75 = bf16[32,512,128]{1,2,0:T(8,128)(2,1)} copy(bf16[32,512,128]{2,1,0:T(8,128)(2,1)} %param.13) | data formatting | bytes 8388608 | tf_op args[0]
  20.6 15.8 %convolution_bitcast_fusion = f32[512,32,512]{0,2,1:T(8,128)} fusion(bf16[32,512,128]{1,2,0:T(8,128)(2,1)} %copy.75, f32[32,512]{1,0:T(8,128)S(1)} %add_rsqrt_fusion.2, f32[32,512]{1,0:T(8,128)S(1)} %broadcast_multiply_fusion.3, bf16[128,640]{1,0:T(8,128)(2,1)S(1)} %copy-done.12), kind=kOutput, calls=%fused_computation.13 | convolution fusion | flops 2155872256 | bytes 38010880 | tf_op jit(solution)/shard_map/ijc,cd->dij/dot_general | solution.py:63
  36.4 15.5 %fusion.15 = (bf16[128,32,512]{0,2,1:T(8,128)(2,1)}, bf16[128,32,512]{0,2,1:T(8,128)(2,1)}) fusion(f32[512,32,512]{0,2,1:T(8,128)} %convolution_bitcast_fusion, f32[32,512]{1,0:T(8,128)S(1)} %broadcast_multiply_fusion), kind=kLoop, calls=%fused_computation.24 | loop fusion | flops 25165824 | bytes 42008576 | tf_op jit(solution)/shard_map/convert_element_type | solution.py:78
  51.9 8.0 %copy.84 = bf16[128,32,512]{2,1,0:T(8,128)(2,1)} copy(bf16[128,32,512]{0,2,1:T(8,128)(2,1)} %get-tuple-element.11) | data formatting | bytes 8388608 | tf_op jit(solution)/shard_map/convert_element_type | solution.py:73
  59.9 6.9 %all-to-all-start = ((bf16[128,32,512]{2,1,0:T(8,128)(2,1)}), bf16[128,32,512]{2,1,0:T(8,128)(2,1)}, u32[]{:S(2)}, u32[]{:S(2)}) async-start(bf16[128,32,512]{2,1,0:T(8,128)(2,1)} %copy.84), calls=%async_computation | async-start | bytes 8388608 | tf_op jit(solution)/shard_map/all_to_all | solution.py:83
  70.6 8.2 %fusion.90 = (bf16[8,512,1024]{2,1,0:T(8,128)(2,1)S(1)}, f32[8,512,1024]{2,1,0:T(8,128)}) fusion(bf16[256,1024]{1,0:T(8,128)(2,1)S(1)} %copy-done, bf16[8,512,256]{1,2,0:T(8,128)(2,1)S(1)} %copy.70, f32[8,512]{1,0:T(8,128)S(1)} %add_rsqrt_fusion.4, f32[8,512]{1,0:T(8,128)S(1)} %broadcast_multiply_fusion.5), kind=kOutput, calls=%fused_computation.117 | convolution fusion | flops 2155872256 | bytes 27820032 | tf_op jit(solution)/shard_map/...c,cd->...d/dot_general | solution.py:17
  97.1 7.9 %copy.86 = bf16[128,32,512]{2,1,0:T(8,128)(2,1)} copy(bf16[128,32,512]{0,2,1:T(8,128)(2,1)} %get-tuple-element.10) | data formatting | bytes 8388608 | tf_op jit(solution)/shard_map/convert_element_type | solution.py:78
  105.1 8.7 %copy.77 = f32[8,512,512]{1,2,0:T(8,128)} copy(bf16[8,512,512]{2,0,1:T(8,128)(2,1)} %all-gather.3.cloned.1.call-done) | data formatting | bytes 12582912 | tf_op jit(solution)/shard_map/convert_element_type | solution.py:125
  113.8 39.5 %fusion.91 = (f32[8,8,512]{2,1,0:T(8,128)S(1)}, f32[8,8,512,512]{2,3,1,0:T(8,128)}) fusion(f32[8,512,512]{1,2,0:T(8,128)} %copy.77, pred[8,512]{1,0:T(8,128)(4,1)S(1)} %get-tuple-element.8, bf16[8,512,8,32]{1,3,2,0:T(8,128)(2,1)} %bitcast.101, bf16[8,512,8,32]{1,3,2,0:T(8,128)(2,1)} %bitcast.102), kind=kOutput, calls=%fused_computation.118 | convolution fusion | flops 1140851200 | bytes 79826944 | tf_op jit(solution)/shard_map/sub | solution.py:129
  153.3 6.6 %all-to-all-done = bf16[128,32,512]{2,1,0:T(8,128)(2,1)} async-done(((bf16[128,32,512]{2,1,0:T(8,128)(2,1)}), bf16[128,32,512]{2,1,0:T(8,128)(2,1)}, u32[]{:S(2)}, u32[]{:S(2)}) %all-to-all-start) | async-done | bytes 4194336 | tf_op jit(solution)/shard_map/all_to_all | solution.py:83
  159.9 5.4 %all-to-all-start.1 = ((bf16[128,32,512]{2,1,0:T(8,128)(2,1)}), bf16[128,32,512]{2,1,0:T(8,128)(2,1)}, u32[]{:S(2)}, u32[]{:S(2)}) async-start(bf16[128,32,512]{2,1,0:T(8,128)(2,1)} %copy.86), calls=%async_computation.1 | async-start | bytes 8388608 | tf_op jit(solution)/shard_map/all_to_all | solution.py:84
  165.3 24.5 %fusion.5 = f32[8,8,32,512]{3,2,1,0:T(8,128)} fusion(bf16[8,512,8,32]{1,3,2,0:T(8,128)(2,1)} %bitcast.110, f32[8,8,512,512]{2,3,1,0:T(8,128)} %get-tuple-element.21, f32[8,8,512]{2,1,0:T(8,128)S(1)} %get-tuple-element.20), kind=kOutput, calls=%fused_computation.10 | convolution fusion | flops 1107296256 | bytes 73531392 | tf_op jit(solution)/shard_map/shij,sjhd->sihd/dot_general | solution.py:130
  189.8 5.3 %copy.79 = f32[8,512,256]{2,1,0:T(8,128)} copy(f32[8,512,256]{1,2,0:T(8,128)} %bitcast.109) | data formatting | bytes 8388608 | tf_op jit(solution)/shard_map/reshape | solution.py:134
  195.2 4.9 copy.85
  200.1 5.8 %fusion.92 = (f32[8,512]{1,0:T(8,128)S(1)}, f32[8,512,256]{1,2,0:T(8,128)}) fusion(bf16[256,256]{1,0:T(8,128)(2,1)S(1)} %copy-done.17, f32[8,512,256]{2,1,0:T(8,128)S(1)} %copy-done.6, f32[8,512,1024]{2,1,0:T(8,128)} %get-tuple-element.19, bf16[8,512,256]{1,2,0:T(8,128)(2,1)S(1)} %copy.70), kind=kOutput, calls=%fused_computation.119 | convolution fusion | flops 545255424 | bytes 14827520 | tf_op jit(solution)/shard_map/...c,cd->...d/dot_general | solution.py:17
  205.9 51.8 %all-to-all-done.1 = bf16[128,32,512]{2,1,0:T(8,128)(2,1)} async-done(((bf16[128,32,512]{2,1,0:T(8,128)(2,1)}), bf16[128,32,512]{2,1,0:T(8,128)(2,1)}, u32[]{:S(2)}, u32[]{:S(2)}) %all-to-all-start.1) | async-done | bytes 4194336 | tf_op jit(solution)/shard_map/all_to_all | solution.py:84
  274.1 5.8 %convolution_convert_fusion = bf16[8,512,512]{2,1,0:T(8,128)(2,1)S(1)} fusion(bf16[8,512,512]{2,1,0:T(8,128)(2,1)} %bitcast.107, bf16[8,512,512]{2,1,0:T(8,128)(2,1)} %bitcast.108), kind=kOutput, calls=%fused_computation.69 | convolution fusion | flops 2149580800 | bytes 12582912 | tf_op jit(solution)/shard_map/cik,cjk->cij/dot_general | solution.py:86
  284.3 6.0 %all-to-all-start.2 = ((bf16[8,512,512]{2,0,1:T(8,128)(2,1)}), bf16[8,512,512]{2,0,1:T(8,128)(2,1)}, u32[]{:S(2)}, u32[]{:S(2)}) async-start(bf16[8,512,512]{2,0,1:T(8,128)(2,1)} %copy.88), calls=%async_computation.2 | async-start | bytes 8388608 | tf_op jit(solution)/shard_map/all_to_all | solution.py:89
  296.2 111.9 %all-to-all-done.2 = bf16[8,512,512]{2,0,1:T(8,128)(2,1)} async-done(((bf16[8,512,512]{2,0,1:T(8,128)(2,1)}), bf16[8,512,512]{2,0,1:T(8,128)(2,1)}, u32[]{:S(2)}, u32[]{:S(2)}) %all-to-all-start.2) | async-done | bytes 4194336 | tf_op jit(solution)/shard_map/all_to_all | solution.py:89
  426.4 20.5 %convert_bitcast_fusion = bf16[32,512,32,32]{1,0,2,3:T(8,128)(2,1)} fusion(bf16[128,32,512,1]{2,1,0,3:T(8,128)(2,1)} %bitcast.103, bf16[128,32,32]{0,2,1:T(8,128)(2,1)S(1)} %copy.97), kind=kOutput, calls=%fused_computation.5 | convolution fusion | flops 4311744512 | bytes 38010880 | tf_op jit(solution)/shard_map/sci,sdj->ijcd/dot_general | solution.py:160
  446.9 31.4 %copy.98 = bf16[32,512,32,32]{1,3,2,0:T(8,128)(2,1)} copy(bf16[32,512,32,32]{1,0,2,3:T(8,128)(2,1)} %convert_bitcast_fusion) | data formatting | bytes 67108864 | tf_op jit(solution)/shard_map/convert_element_type | solution.py:22
  478.3 14.3 %fusion.6 = f32[32,512,128]{1,2,0:T(8,128)} fusion(f32[32,512,128]{1,2,0:T(8,128)} %copy-done.5, f32[32,512]{1,0:T(8,128)S(1)} %add_rsqrt_fusion, f32[32,512]{1,0:T(8,128)S(1)} %broadcast_multiply_fusion.1, bf16[512,128]{1,0:T(8,128)(2,1)S(1)} %copy-done.18, bf16[128,512]{1,0:T(8,128)(2,1)S(1)} %copy-done.19), kind=kOutput, calls=%fused_computation.11 | convolution fusion | flops 4318035968 | bytes 17170432 | tf_op jit(solution)/shard_map/...c,cd->...d/dot_general | solution.py:17
  492.6 20.1 %add_convert_fusion = bf16[32,512,128]{1,2,0:T(8,128)(2,1)} fusion(f32[32,512,128]{1,2,0:T(8,128)} %copy-done.5, f32[32,512,128]{1,2,0:T(8,128)} %fusion.6, f32[32,512]{1,0:T(8,128)S(1)} %convolution_maximum_fusion, bf16[32,512,1024]{1,2,0:T(8,128)(2,1)} %bitcast.100, bf16[1024,128]{1,0:T(8,128)(2,1)S(1)} %copy-done.16), kind=kOutput, calls=%fused_computation.40 | convolution fusion | flops 4303355904 | bytes 54853632 | tf_op jit(solution)/shard_map/...c,cd->...d/dot_general | solution.py:17
  512.7 6.4 %copy.102 = bf16[32,512,128]{2,1,0:T(8,128)(2,1)} copy(bf16[32,512,128]{1,2,0:T(8,128)(2,1)} %add_convert_fusion) | data formatting | bytes 8388608
  (93 shorter events, 73.8 us)
Async XLA Ops:
  7.2 63.4 %copy-start = (bf16[256,1024]{1,0:T(8,128)(2,1)S(1)}, bf16[256,1024]{1,0:T(8,128)(2,1)}, u32[]{:S(2)}) copy-start(bf16[256,1024]{1,0:T(8,128)(2,1)} %param.18) | copy-start | bytes 1572868
  7.2 97.9 %all-gather.3.cloned.1.call-start = ((), (), s32[]{:S(2)}) async-start(), calls=%async_computation.4 | async-start | bytes 4456448 | tf_op jit(solution)/shard_map/all_gather | solution.py:120
  13.7 3.4 copy-start.2
  13.7 4.8 copy-start.20
  17.1 3.4 copy-start.7
  18.6 17.8 %copy-start.9 = (f32[32,512]{1,0:T(8,128)}, f32[32,512]{1,0:T(8,128)S(1)}, u32[]{:S(2)}) copy-start(f32[32,512]{1,0:T(8,128)S(1)} %add_rsqrt_fusion.2) | copy-start | bytes 196612
  59.9 100.1 %all-to-all-start = ((bf16[128,32,512]{2,1,0:T(8,128)(2,1)}), bf16[128,32,512]{2,1,0:T(8,128)(2,1)}, u32[]{:S(2)}, u32[]{:S(2)}) async-start(bf16[128,32,512]{2,1,0:T(8,128)(2,1)} %copy.84), calls=%async_computation | async-start | bytes 8388608 | tf_op jit(solution)/shard_map/all_to_all | solution.py:83
  97.1 7.9 %copy-start.11 = (s32[128,512]{1,0:T(8,128)S(1)}, s32[128,512]{1,0:T(8,128)}, u32[]{:S(2)}) copy-start(s32[128,512]{1,0:T(8,128)} %param.15) | copy-start | bytes 786436
  159.9 97.7 %all-to-all-start.1 = ((bf16[128,32,512]{2,1,0:T(8,128)(2,1)}), bf16[128,32,512]{2,1,0:T(8,128)(2,1)}, u32[]{:S(2)}, u32[]{:S(2)}) async-start(bf16[128,32,512]{2,1,0:T(8,128)(2,1)} %copy.86), calls=%async_computation.1 | async-start | bytes 8388608 | tf_op jit(solution)/shard_map/all_to_all | solution.py:84
  195.2 4.9 copy-start.6
  195.2 4.9 copy-start.17
  257.6 4.9 copy-start.4
  269.4 15.0 %all-to-all-start.3 = ((bf16[16,2,4096]{2,1,0:T(2,128)(2,1)}), bf16[16,2,4096]{2,1,0:T(2,128)(2,1)S(1)}, u32[]{:S(2)}, u32[]{:S(2)}) async-start(bf16[16,2,4096]{2,1,0:T(2,128)(2,1)} %reshape.139), calls=%async_computation.3 | async-start | bytes 524288 | tf_op jit(solution)/shard_map/all_to_all | solution.py:158
  284.3 123.8 %all-to-all-start.2 = ((bf16[8,512,512]{2,0,1:T(8,128)(2,1)}), bf16[8,512,512]{2,0,1:T(8,128)(2,1)}, u32[]{:S(2)}, u32[]{:S(2)}) async-start(bf16[8,512,512]{2,0,1:T(8,128)(2,1)} %copy.88), calls=%async_computation.2 | async-start | bytes 8388608 | tf_op jit(solution)/shard_map/all_to_all | solution.py:89
  290.3 136.0 %all-gather.5.cloned.1.call-start = ((), (), s32[]{:S(2)}) async-start(), calls=%async_computation.5 | async-start | bytes 4456448 | tf_op jit(solution)/shard_map/all_gather | solution.py:159
  408.1 6.3 %copy-start.14 = (bf16[128,128]{1,0:T(8,128)(2,1)S(1)}, bf16[128,128]{1,0:T(8,128)(2,1)}, u32[]{:S(2)}) copy-start(bf16[128,128]{1,0:T(8,128)(2,1)} %param.23) | copy-start | bytes 98308
  414.4 3.9 copy-start.3
  414.4 3.9 copy-start.8
  414.4 3.9 copy-start.10
  423.1 3.2 copy-start.5
  446.9 31.4 %copy-start.18 = (bf16[512,128]{1,0:T(8,128)(2,1)S(1)}, bf16[512,128]{1,0:T(8,128)(2,1)}, u32[]{:S(2)}) copy-start(bf16[512,128]{1,0:T(8,128)(2,1)} %param.25) | copy-start | bytes 393220
  446.9 31.4 %copy-start.19 = (bf16[128,512]{1,0:T(8,128)(2,1)S(1)}, bf16[128,512]{1,0:T(8,128)(2,1)}, u32[]{:S(2)}) copy-start(bf16[128,512]{1,0:T(8,128)(2,1)} %param.24) | copy-start | bytes 393220
  478.3 14.3 %copy-start.16 = (bf16[1024,128]{1,0:T(8,128)(2,1)S(1)}, bf16[1024,128]{1,0:T(8,128)(2,1)}, u32[]{:S(2)}) copy-start(bf16[1024,128]{1,0:T(8,128)(2,1)} %param.21) | copy-start | bytes 786436
  492.6 26.5 %copy-start.1 = (bf16[256,1024]{1,0:T(8,128)(2,1)S(1)}, bf16[256,1024]{1,0:T(8,128)(2,1)}, u32[]{:S(2)}) copy-start(bf16[256,1024]{1,0:T(8,128)(2,1)} %param.18) | copy-start | bytes 1572868
  (3 other events, 4.7 us)
Sparse Core Ops, SparseCore 0:
  20.5 51.1 all-gather.2
  293.3 94.7 all-gather.4
where the time goes:
time: 534 us; the launch traced here: 526 us
  waiting for transfers between devices  171 us (32%)
  matrix products  166 us (31%)
  local copies, waits for them, and re-layouts  118 us (22%)
  other arithmetic  33.3 us (6%)
  starting transfers between devices  23.6 us (4%)
  between operations  14.6 us (3%)
    all_to_all x1, waiting for transfers between devices, body(): lax.all_to_all(tri_sum, 'row', split_axis=1, concat_axis=0, tiled=True)  112 us
    dot_general x5, matrix products, apply_matrix_map(): jnp.einsum('...c,cd->...d', values, weight, preferred_element_type=jnp.fl...  53.1 us
    all_to_all x1, waiting for transfers between devices, body(): lax.all_to_all(right_tri, 'row', split_axis=0, concat_axis=1, tiled=True)  51.8 us
    sub x1, matrix products, body(): attn_weights = jax.nn.softmax(affinity_matrix, axis=-1).astype(jnp.bfloat16)  39.5 us
    convert_element_type x1, local copies, waits for them, and re-layouts, project_outer(): raw_outer.astype(jnp.bfloat16)  31.4 us
    dot_general x1, matrix products, body(): jnp.einsum('shij,sjhd->sihd', attn_weights, content_subspaces, preferred_...  24.5 us
    unnamed x48, local copies, waits for them, and re-layouts  24 us
    dot_general x1, matrix products, body(): jnp.einsum('sci,sdj->ijcd', left_res, right_all, preferred_element_type=j...  20.5 us
  transfers between devices with their start and end apart: 6, of which 3 were waited for; matrix products, arithmetic and copies ran while one was open for 38% of the time, Pallas kernels for 0%

commit v1 on v0

--- a/solution.py
+++ b/solution.py
@@ -81,7 +81,12 @@
     )
     left_full, right_full = (
         lax.all_to_all(left_tri, "row", split_axis=0, concat_axis=1, tiled=True),
-        lax.all_to_all(right_tri, "row", split_axis=0, concat_axis=1, tiled=True),
+        jnp.concatenate(
+            lax.all_to_all(
+                jnp.stack(jnp.split(right_tri, lax.axis_size("row"), axis=0)), "row", 0, 0
+            ),
+            axis=1,
+        ),
     )
     tri_sum = jnp.einsum(
         "cik,cjk->cij", left_full, right_full, preferred_element_type=jnp.float32

time: 534 us -> 526 us (0.985)
  waiting for transfers between devices: 171 us -> 159 us
    unnamed x48 -> x63, local copies, waits for them, and re-layouts: 24 us -> 41.6 us
    convert_element_type x1 -> x0, local copies, waits for them, and re-layouts: 7.92 us -> none  [body(): right_tri = (jax.nn.sigmoid(tri_gates[2 * pair_width:3 * pair_width]) * t...]
    all_to_all x1, waiting for transfers between devices: 6.6 us -> 0.01 us  [body(): lax.all_to_all(left_tri, 'row', split_axis=0, concat_axis=1, tiled=True)]
  transfers between devices with their start and end apart: 6 -> 6, of which waited for: 3 -> 2; matrix products, arithmetic and copies ran while one was open for 38% -> 41% of each run, Pallas kernels for 0% -> 0%
where the time goes in v1:
time: 526 us; the launch traced here: 516 us
  matrix products  164 us (31%)
  waiting for transfers between devices  159 us (30%)
  local copies, waits for them, and re-layouts  120 us (23%)
  other arithmetic  33.4 us (6%)
  starting transfers between devices  24.5 us (5%)
  between operations  14.7 us (3%)
    all_to_all x1, waiting for transfers between devices, body(): lax.all_to_all(tri_sum, 'row', split_axis=1, concat_axis=0, tiled=True)  112 us
    dot_general x5, matrix products, apply_matrix_map(): jnp.einsum('...c,cd->...d', values, weight, preferred_element_type=jnp.fl...  51.1 us
    all_to_all x1, waiting for transfers between devices, body(): lax.all_to_all(jnp.stack(jnp.split(right_tri, lax.axis_size('row'), axis=...  46.9 us
    unnamed x63, local copies, waits for them, and re-layouts  41.6 us
    sub x1, matrix products, body(): attn_weights = jax.nn.softmax(affinity_matrix, axis=-1).astype(jnp.bfloat16)  39.5 us
    convert_element_type x1, local copies, waits for them, and re-layouts, project_outer(): raw_outer.astype(jnp.bfloat16)  31.4 us
    dot_general x1, matrix products, body(): jnp.einsum('shij,sjhd->sihd', attn_weights, content_subspaces, preferred_...  24.5 us
    dot_general x1, matrix products, body(): jnp.einsum('sci,sdj->ijcd', left_res, right_all, preferred_element_type=j...  20.5 us
  transfers between devices with their start and end apart: 6, of which 2 were waited for; matrix products, arithmetic and copies ran while one was open for 41% of the time, Pallas kernels for 0%

profile of v1, /device:TPU:13, one launch (start us, length us, event | category | flops | bytes accessed | tf_op | source)
XLA Modules:
  0.0 516.0 jit_solution(5639634824024660918)
XLA Ops:
  7.2 6.5 %copy.75 = bf16[32,512,128]{1,2,0:T(8,128)(2,1)} copy(bf16[32,512,128]{2,1,0:T(8,128)(2,1)} %param.13) | data formatting | bytes 8388608 | tf_op args[0]
  20.4 15.7 %convolution_bitcast_fusion = f32[512,32,512]{2,0,1:T(8,128)} fusion(bf16[32,512,128]{1,2,0:T(8,128)(2,1)} %copy.75, f32[32,512]{1,0:T(8,128)S(1)} %add_rsqrt_fusion.2, f32[32,512]{1,0:T(8,128)S(1)} %broadcast_multiply_fusion.3, bf16[128,640]{1,0:T(8,128)(2,1)S(1)} %copy-done.12), kind=kOutput, calls=%fused_computation.13 | convolution fusion | flops 2155872256 | bytes 38010880 | tf_op jit(solution)/shard_map/ijc,cd->dij/dot_general | solution.py:63
  36.2 15.6 %fusion.15 = (bf16[128,32,512]{2,0,1:T(8,128)(2,1)}, bf16[128,32,512]{2,0,1:T(8,128)(2,1)S(1)}) fusion(f32[512,32,512]{2,0,1:T(8,128)} %convolution_bitcast_fusion, f32[32,512]{1,0:T(8,128)S(1)} %broadcast_multiply_fusion), kind=kLoop, calls=%fused_computation.24 | loop fusion | flops 25165824 | bytes 42008576 | tf_op jit(solution)/shard_map/convert_element_type | solution.py:78
  51.8 4.4 copy.85
  56.2 6.9 %all-to-all-start = ((bf16[128,32,512]{2,1,0:T(8,128)(2,1)}), bf16[128,32,512]{2,1,0:T(8,128)(2,1)}, u32[]{:S(2)}, u32[]{:S(2)}) async-start(bf16[128,32,512]{2,1,0:T(8,128)(2,1)} %copy.85), calls=%async_computation | async-start | bytes 8388608 | tf_op jit(solution)/shard_map/all_to_all | solution.py:83
  66.8 8.2 %fusion.111 = (bf16[8,512,1024]{2,1,0:T(8,128)(2,1)S(1)}, f32[8,512,1024]{2,1,0:T(8,128)}) fusion(bf16[256,1024]{1,0:T(8,128)(2,1)S(1)} %copy-done, bf16[8,512,256]{1,2,0:T(8,128)(2,1)S(1)} %copy.70, f32[8,512]{1,0:T(8,128)S(1)} %add_rsqrt_fusion.4, f32[8,512]{1,0:T(8,128)S(1)} %broadcast_multiply_fusion.5), kind=kOutput, calls=%fused_computation.151 | convolution fusion | flops 2155872256 | bytes 27820032 | tf_op jit(solution)/shard_map/...c,cd->...d/dot_general | solution.py:17
  111.8 8.7 %copy.77 = f32[8,512,512]{1,2,0:T(8,128)} copy(bf16[8,512,512]{2,0,1:T(8,128)(2,1)} %all-gather.3.cloned.1.call-done) | data formatting | bytes 12582912 | tf_op jit(solution)/shard_map/convert_element_type | solution.py:130
  120.5 39.5 %fusion.112 = (f32[8,8,512]{2,1,0:T(8,128)S(1)}, f32[8,8,512,512]{2,3,1,0:T(8,128)}) fusion(f32[8,512,512]{1,2,0:T(8,128)} %copy.77, pred[8,512]{1,0:T(8,128)(4,1)S(1)} %get-tuple-element.8, bf16[8,512,8,32]{1,3,2,0:T(8,128)(2,1)} %bitcast.164, bf16[8,512,8,32]{1,3,2,0:T(8,128)(2,1)} %bitcast.165), kind=kOutput, calls=%fused_computation.152 | convolution fusion | flops 1140851200 | bytes 79826944 | tf_op jit(solution)/shard_map/sub | solution.py:134
  160.0 6.4 %all-to-all-start.1 = ((bf16[16,8,32,512]{3,1,2,0:T(8,128)(2,1)}), bf16[16,8,32,512]{3,1,2,0:T(8,128)(2,1)}, u32[]{:S(2)}, u32[]{:S(2)}) async-start(bf16[16,8,32,512]{3,1,2,0:T(8,128)(2,1)} %fusion.75), calls=%async_computation.1 | async-start | bytes 8388608 | tf_op jit(solution)/shard_map/all_to_all | solution.py:85
  166.4 24.5 %fusion.5 = f32[8,8,32,512]{3,2,1,0:T(8,128)} fusion(bf16[8,512,8,32]{1,3,2,0:T(8,128)(2,1)} %bitcast.172, f32[8,8,512,512]{2,3,1,0:T(8,128)} %get-tuple-element.21, f32[8,8,512]{2,1,0:T(8,128)S(1)} %get-tuple-element.20), kind=kOutput, calls=%fused_computation.10 | convolution fusion | flops 1107296256 | bytes 73531392 | tf_op jit(solution)/shard_map/shij,sjhd->sihd/dot_general | solution.py:135
  190.9 5.3 %copy.79 = f32[8,512,256]{2,1,0:T(8,128)} copy(f32[8,512,256]{1,2,0:T(8,128)} %bitcast.171) | data formatting | bytes 8388608 | tf_op jit(solution)/shard_map/reshape | solution.py:139
  196.2 4.9 copy.86
  211.7 46.9 %all-to-all-done.1 = bf16[16,8,32,512]{3,1,2,0:T(8,128)(2,1)} async-done(((bf16[16,8,32,512]{3,1,2,0:T(8,128)(2,1)}), bf16[16,8,32,512]{3,1,2,0:T(8,128)(2,1)}, u32[]{:S(2)}, u32[]{:S(2)}) %all-to-all-start.1) | async-done | bytes 4194336 | tf_op jit(solution)/shard_map/all_to_all | solution.py:85
  258.7 4.8 all-to-all-start.3
  263.5 6.4 %fusion.50 = bf16[8,512,512]{2,1,0:T(8,128)(2,1)S(1)} fusion(bf16[8,512,512]{2,1,0:T(8,128)(2,1)} %bitcast.170, bf16[8,512,512]{2,0,1:T(8,128)(2,1)} %bitcast.32), kind=kOutput, calls=%fused_computation.71 | convolution fusion | flops 2149580800 | bytes 12582912 | tf_op jit(solution)/shard_map/cik,cjk->cij/dot_general | solution.py:91
  269.9 4.4 copy.88
  274.2 6.0 %all-to-all-start.2 = ((bf16[8,512,512]{2,0,1:T(8,128)(2,1)}), bf16[8,512,512]{2,0,1:T(8,128)(2,1)}, u32[]{:S(2)}, u32[]{:S(2)}) async-start(bf16[8,512,512]{2,0,1:T(8,128)(2,1)} %copy.88), calls=%async_computation.2 | async-start | bytes 8388608 | tf_op jit(solution)/shard_map/all_to_all | solution.py:94
  286.1 111.9 %all-to-all-done.2 = bf16[8,512,512]{2,0,1:T(8,128)(2,1)} async-done(((bf16[8,512,512]{2,0,1:T(8,128)(2,1)}), bf16[8,512,512]{2,0,1:T(8,128)(2,1)}, u32[]{:S(2)}, u32[]{:S(2)}) %all-to-all-start.2) | async-done | bytes 4194336 | tf_op jit(solution)/shard_map/all_to_all | solution.py:94
  408.3 4.7 fusion.114
  416.3 20.5 %convert_bitcast_fusion = bf16[32,512,32,32]{1,0,2,3:T(8,128)(2,1)} fusion(bf16[128,32,512,1]{2,1,0,3:T(8,128)(2,1)} %bitcast.166, bf16[128,32,32]{0,2,1:T(8,128)(2,1)S(1)} %copy.97), kind=kOutput, calls=%fused_computation.5 | convolution fusion | flops 4311744512 | bytes 38010880 | tf_op jit(solution)/shard_map/sci,sdj->ijcd/dot_general | solution.py:165
  436.8 31.4 %copy.98 = bf16[32,512,32,32]{1,3,2,0:T(8,128)(2,1)} copy(bf16[32,512,32,32]{1,0,2,3:T(8,128)(2,1)} %convert_bitcast_fusion) | data formatting | bytes 67108864 | tf_op jit(solution)/shard_map/convert_element_type | solution.py:22
  468.2 14.3 %fusion.6 = f32[32,512,128]{1,2,0:T(8,128)} fusion(f32[32,512,128]{1,2,0:T(8,128)} %copy-done.5, f32[32,512]{1,0:T(8,128)S(1)} %add_rsqrt_fusion, f32[32,512]{1,0:T(8,128)S(1)} %broadcast_multiply_fusion.1, bf16[512,128]{1,0:T(8,128)(2,1)S(1)} %copy-done.18, bf16[128,512]{1,0:T(8,128)(2,1)S(1)} %copy-done.19), kind=kOutput, calls=%fused_computation.11 | convolution fusion | flops 4318035968 | bytes 17170432 | tf_op jit(solution)/shard_map/...c,cd->...d/dot_general | solution.py:17
  482.5 20.1 %add_convert_fusion = bf16[32,512,128]{1,2,0:T(8,128)(2,1)} fusion(f32[32,512,128]{1,2,0:T(8,128)} %copy-done.5, f32[32,512,128]{1,2,0:T(8,128)} %fusion.6, f32[32,512]{1,0:T(8,128)S(1)} %convolution_maximum_fusion, bf16[32,512,1024]{1,2,0:T(8,128)(2,1)} %bitcast.163, bf16[1024,128]{1,0:T(8,128)(2,1)S(1)} %copy-done.16), kind=kOutput, calls=%fused_computation.40 | convolution fusion | flops 4303355904 | bytes 54853632 | tf_op jit(solution)/shard_map/...c,cd->...d/dot_general | solution.py:17
  502.6 6.4 %copy.102 = bf16[32,512,128]{2,1,0:T(8,128)(2,1)} copy(bf16[32,512,128]{1,2,0:T(8,128)(2,1)} %add_convert_fusion) | data formatting | bytes 8388608
  (107 shorter events, 77.1 us)
Async XLA Ops:
  7.2 59.7 %copy-start = (bf16[256,1024]{1,0:T(8,128)(2,1)S(1)}, bf16[256,1024]{1,0:T(8,128)(2,1)}, u32[]{:S(2)}) copy-start(bf16[256,1024]{1,0:T(8,128)(2,1)} %param.18) | copy-start | bytes 1572868
  7.2 104.6 %all-gather.3.cloned.1.call-start = ((), (), s32[]{:S(2)}) async-start(), calls=%async_computation.4 | async-start | bytes 4456448 | tf_op jit(solution)/shard_map/all_gather | solution.py:125
  13.7 3.4 copy-start.2
  13.7 4.8 copy-start.20
  17.1 3.2 copy-start.7
  18.6 17.5 %copy-start.9 = (f32[32,512]{1,0:T(8,128)}, f32[32,512]{1,0:T(8,128)S(1)}, u32[]{:S(2)}) copy-start(f32[32,512]{1,0:T(8,128)S(1)} %add_rsqrt_fusion.2) | copy-start | bytes 196612
  56.2 103.8 %all-to-all-start = ((bf16[128,32,512]{2,1,0:T(8,128)(2,1)}), bf16[128,32,512]{2,1,0:T(8,128)(2,1)}, u32[]{:S(2)}, u32[]{:S(2)}) async-start(bf16[128,32,512]{2,1,0:T(8,128)(2,1)} %copy.85), calls=%async_computation | async-start | bytes 8388608 | tf_op jit(solution)/shard_map/all_to_all | solution.py:83
  85.4 7.9 %copy-start.11 = (s32[128,512]{1,0:T(8,128)S(1)}, s32[128,512]{1,0:T(8,128)}, u32[]{:S(2)}) copy-start(s32[128,512]{1,0:T(8,128)} %param.15) | copy-start | bytes 786436
  93.4 11.9 %copy-start.4 = (bf16[128,32,512]{2,0,1:T(8,128)(2,1)S(1)}, bf16[128,32,512]{2,0,1:T(8,128)(2,1)}, u32[]{:S(2)}) copy-start(bf16[128,32,512]{2,0,1:T(8,128)(2,1)} %get-tuple-element.10) | copy-start | bytes 12582916
  160.0 98.7 %all-to-all-start.1 = ((bf16[16,8,32,512]{3,1,2,0:T(8,128)(2,1)}), bf16[16,8,32,512]{3,1,2,0:T(8,128)(2,1)}, u32[]{:S(2)}, u32[]{:S(2)}) async-start(bf16[16,8,32,512]{3,1,2,0:T(8,128)(2,1)} %fusion.75), calls=%async_computation.1 | async-start | bytes 8388608 | tf_op jit(solution)/shard_map/all_to_all | solution.py:85
  196.2 4.9 copy-start.6
  196.2 4.9 copy-start.17
  258.7 15.5 %all-to-all-start.3 = ((bf16[16,2,4096]{2,1,0:T(2,128)(2,1)}), bf16[16,2,4096]{2,1,0:T(2,128)(2,1)S(1)}, u32[]{:S(2)}, u32[]{:S(2)}) async-start(bf16[16,2,4096]{2,1,0:T(2,128)(2,1)} %reshape.147), calls=%async_computation.3 | async-start | bytes 524288 | tf_op jit(solution)/shard_map/all_to_all | solution.py:163
  274.2 123.8 %all-to-all-start.2 = ((bf16[8,512,512]{2,0,1:T(8,128)(2,1)}), bf16[8,512,512]{2,0,1:T(8,128)(2,1)}, u32[]{:S(2)}, u32[]{:S(2)}) async-start(bf16[8,512,512]{2,0,1:T(8,128)(2,1)} %copy.88), calls=%async_computation.2 | async-start | bytes 8388608 | tf_op jit(solution)/shard_map/all_to_all | solution.py:94
  280.2 136.0 %all-gather.5.cloned.1.call-start = ((), (), s32[]{:S(2)}) async-start(), calls=%async_computation.5 | async-start | bytes 4456448 | tf_op jit(solution)/shard_map/all_gather | solution.py:164
  398.0 6.3 %copy-start.14 = (bf16[128,128]{1,0:T(8,128)(2,1)S(1)}, bf16[128,128]{1,0:T(8,128)(2,1)}, u32[]{:S(2)}) copy-start(bf16[128,128]{1,0:T(8,128)(2,1)} %param.23) | copy-start | bytes 98308
  404.3 3.9 copy-start.3
  404.3 3.9 copy-start.8
  404.3 3.9 copy-start.10
  413.0 3.2 copy-start.5
  436.8 31.4 %copy-start.18 = (bf16[512,128]{1,0:T(8,128)(2,1)S(1)}, bf16[512,128]{1,0:T(8,128)(2,1)}, u32[]{:S(2)}) copy-start(bf16[512,128]{1,0:T(8,128)(2,1)} %param.25) | copy-start | bytes 393220
  436.8 31.4 %copy-start.19 = (bf16[128,512]{1,0:T(8,128)(2,1)S(1)}, bf16[128,512]{1,0:T(8,128)(2,1)}, u32[]{:S(2)}) copy-start(bf16[128,512]{1,0:T(8,128)(2,1)} %param.24) | copy-start | bytes 393220
  468.2 14.4 %copy-start.16 = (bf16[1024,128]{1,0:T(8,128)(2,1)S(1)}, bf16[1024,128]{1,0:T(8,128)(2,1)}, u32[]{:S(2)}) copy-start(bf16[1024,128]{1,0:T(8,128)(2,1)} %param.21) | copy-start | bytes 786436
  482.5 26.5 %copy-start.1 = (bf16[256,1024]{1,0:T(8,128)(2,1)S(1)}, bf16[256,1024]{1,0:T(8,128)(2,1)}, u32[]{:S(2)}) copy-start(bf16[256,1024]{1,0:T(8,128)(2,1)} %param.18) | copy-start | bytes 1572868
  (3 other events, 4.5 us)
Sparse Core Ops, SparseCore 0:
  20.5 54.6 all-gather.2
  283.2 94.7 all-gather.4
